TPU v7x, 256 devices: a whole 4x4x8 slice. The times are simulated.
256 devices in a mesh: replica: 16 (over z_hi, y), tensor: 16 (over x, z_lo, core).
Axes of the slice: x: 4, y: 4, z: 8 (z_hi: 4, z_lo: 2; z = z_hi * 2 + z_lo), core: 2. Of those that a mesh axis runs over, the one named last changes fastest.
Arguments:
- activations: bfloat16 [16384, 2048], P('replica', 'tensor'), may hold values from -0.625 to 0.625
- grad_out: bfloat16 [16384, 7168], P('replica', 'tensor'), may hold values from -6 to 6
- weight: bfloat16 [2048, 7168], P(None, 'tensor'), may hold values from -0.0625 to 0.0625
- momentum: float32 [16, 2048, 7168], P('replica', None, 'tensor'), may hold values from -6 to 6
- freq_rows: int32 [16, 32, 112], P(None, None, 'tensor'), may hold values from 0 to 63
Outputs:
- input_grad: bfloat16 [16384, 2048], P('replica', 'tensor')
- momentum_out: float32 [16, 2048, 7168], P('replica', None, 'tensor')
- update: bfloat16 [2048, 7168], P(None, 'tensor')
All inputs are finite; a program needn't handle non-finite values.
Results may differ from a plain program's by a relative error of at most 0.001.
Values may be sent and summed in bfloat16 or wider, within the bound.
A program may use at most 128 MiB of HBM per device.

v0:
```python
import jax
import jax.numpy as jnp
from jax import lax
from jax.sharding import PartitionSpec as P

TILE = 64
decay_rate = 0.9
highest = lax.Precision.HIGHEST


def cosine_table():
    freq = jnp.arange(TILE, dtype=jnp.float32)[:, None]
    place = jnp.arange(TILE, dtype=jnp.float32)[None, :]
    values = jnp.cos(jnp.pi * (2.0 * place + 1.0) * freq / (2.0 * TILE)) * jnp.sqrt(2.0 / TILE)
    return jnp.where(freq == 0.0, values / jnp.sqrt(2.0), values)


def decode(coeff_all, chosen_all, basis):
    onehot = (chosen_all[..., None] == jnp.arange(TILE, dtype=jnp.int32)).astype(jnp.float32)
    summed = jnp.einsum("rack,racj->ackj", onehot, coeff_all, precision=highest)
    right_done = jnp.einsum("ackj,jm->ackm", summed, basis, precision=highest)
    decoded = jnp.einsum("kn,ackm->ancm", basis, right_done, precision=highest)
    return decoded.reshape(summed.shape[0] * TILE, summed.shape[1] * TILE)


def body(activations, grad_out, weight, momentum, freq_rows):
    basis = cosine_table()
    partial_value = lax.dot_general(
        grad_out, weight, (((1,), (1,)), ((), ())), preferred_element_type=jnp.float32
    )
    input_grad = lax.psum_scatter(partial_value, "tensor", scatter_dimension=1, tiled=True).astype(
        jnp.bfloat16
    )
    weight_grad = lax.dot_general(
        lax.all_gather(activations, "tensor", axis=1, tiled=True),
        grad_out,
        (((0,), (0,)), ((), ())),
        preferred_element_type=jnp.float32,
    )
    feature_count = weight_grad.shape[0]
    hidden_count = weight_grad.shape[1]
    tile_rows = feature_count // TILE
    tile_cols = hidden_count // TILE
    kept = decay_rate * momentum[0] + weight_grad
    my_index = lax.axis_index("replica")
    chosen = lax.dynamic_index_in_dim(freq_rows, my_index, 0, keepdims=False)
    tile_view = kept.reshape(tile_rows, TILE, tile_cols, TILE)
    half_done = jnp.einsum("ancm,lm->ancl", tile_view, basis, precision=highest)
    onehot = (chosen[:, :, None] == jnp.arange(TILE, dtype=jnp.int32)[None, None, :]).astype(
        jnp.float32
    )
    picked = jnp.einsum("ack,kn->acn", onehot, basis, precision=highest)
    coeff_rows = jnp.einsum("acn,ancl->acl", picked, half_done, precision=highest)
    spread = jnp.einsum("acj,jm->acm", coeff_rows, basis, precision=highest)
    removed = jnp.einsum("acn,acm->ancm", picked, spread)
    momentum_out = (kept - removed.reshape(feature_count, hidden_count))[None]
    band = tile_rows // 4
    results = []
    for block_index in range(4):
        block_rows = coeff_rows[block_index * band : (block_index + 1) * band]
        gathered = lax.all_gather(block_rows[None], "replica", axis=0, tiled=True)
        block_chosen = freq_rows[:, block_index * band : (block_index + 1) * band]
        results.append(decode(gathered, block_chosen, basis))
    update = jnp.concatenate(results, axis=0).astype(jnp.bfloat16)
    return (input_grad, momentum_out, update)


def solution(mesh):
    placed = (
        P("replica", "tensor"),
        P("replica", "tensor"),
        P(None, "tensor"),
        P("replica", None, "tensor"),
        P(None, None, "tensor"),
    )
    return jax.shard_map(
        body,
        mesh=mesh,
        in_specs=placed,
        out_specs=(P("replica", "tensor"), P("replica", None, "tensor"), P(None, "tensor")),
        check_vma=False,
    )
```

profile of v0, /device:TPU:8, one launch (start us, length us, event | category | flops | bytes accessed | tf_op | source)
XLA Modules:
  0.0 345.8 jit_solution(10398331758102312585)
XLA Ops:
  7.2 0.7 all-gather.6.cloned.1.call-update
  8.0 0.7 copy-done
  8.7 6.8 %fusion.128 = f32[1024,2048]{1,0:T(8,128)} fusion(bf16[1024,448]{0,1:T(8,128)(2,1)} %param.6, bf16[2048,448]{0,1:T(8,128)(2,1)S(1)} %copy-done), kind=kOutput, calls=%fused_computation.147 | convolution fusion | flops 1879048192 | bytes 11141120 | tf_op jit(solution)/shard_map/dot_general | solution.py:28
  15.5 0.8 copy-done.3
  18.3 41.7 %all-gather.6.cloned.1.call-done = bf16[1024,2048]{1,0:T(8,128)(2,1)} async-done(((bf16[1024,128]{1,0:T(8,128)(2,1)}), bf16[1024,2048]{1,0:T(8,128)(2,1)}) %all-gather.6.cloned.1.call-update) | async-done | bytes 4194320 | tf_op jit(solution)/shard_map/all_gather | solution.py:35
  59.9 7.3 %bitcast_add_fusion = f32[2048,448]{0,1:T(8,128)} fusion(f32[1,2048,448]{1,2,0:T(8,128)} %param.8, bf16[1024,448]{0,1:T(8,128)(2,1)S(1)} %copy-done.6, bf16[1024,2048]{1,0:T(8,128)(2,1)} %all-gather.6.cloned.1.call-done), kind=kOutput, calls=%fused_computation.3 | convolution fusion | flops 1880883200 | bytes 12451840 | tf_op jit(solution)/shard_map/dot_general | solution.py:34
  67.2 7.9 %reshape.50 = f32[32,64,7,64]{1,0,3,2:T(8,128)} reshape(f32[2048,448]{0,1:T(8,128)} %bitcast_add_fusion) | data formatting | bytes 7340032 | tf_op jit(solution)/shard_map/reshape | solution.py:47
  75.1 16.1 %fusion = f32[32,64,7,64]{3,1,2,0:T(8,128)S(1)} fusion(f32[32,64,7,64]{1,0,3,2:T(8,128)} %reshape.50, f32[64]{0:T(128)S(1)} %add_multiply_fusion, pred[64]{0:T(512)(128)(4,1)S(1)} %iota_compare_fusion.6), kind=kOutput, calls=%fused_computation | convolution fusion | flops 704663552 | bytes 7340352 | tf_op jit(solution)/shard_map/ancm,lm->ancl/dot_general | solution.py:48
  91.2 6.2 %fusion.18 = f32[32,7,1,64]{3,2,1,0:T(1,128)S(1)} fusion(f32[32,64,7,64]{3,1,2,0:T(8,128)S(1)} %fusion, f32[32,7,64,1]{2,0,1,3:T(8,128)S(1)} %bitcast.92), kind=kOutput, calls=%fused_computation.31 | convolution fusion | flops 11010048 | bytes 3784704 | tf_op jit(solution)/shard_map/acn,ancl->acl/dot_general | solution.py:53
  97.5 46.7 %all-gather = f32[128,7,64]{2,0,1:T(8,128)S(1)} all-gather(f32[8,7,64]{2,0,1:T(8,128)S(1)} %get-tuple-element.3), channel_id=2, replica_groups=mesh['replica'=16,'tensor'=16] {'replica'}, dimensions={0}, use_global_device_ids=true | all-gather | bytes 243712 | tf_op jit(solution)/shard_map/all_gather | solution.py:61
  144.2 1.6 fusion.12
  145.8 5.4 %fusion.32 = f32[8,7,64,64]{2,3,1,0:T(8,128)S(1)} fusion(f32[8,7,64,64]{3,2,1,0:T(8,128)S(1)} %fusion.12, f32[64]{0:T(128)S(1)} %add_multiply_fusion, pred[64]{0:T(512)(128)(4,1)S(1)} %iota_compare_fusion.6), kind=kOutput, calls=%fused_computation.46 | convolution fusion | flops 176181248 | bytes 1835328 | tf_op jit(solution)/shard_map/ackj,jm->ackm/dot_general | solution.py:21
  151.2 1.7 fusion.2
  154.1 48.2 %all-gather.1 = f32[128,7,64]{2,0,1:T(8,128)S(1)} all-gather(f32[8,7,64]{2,0,1:T(8,128)S(1)} %get-tuple-element.5), channel_id=3, replica_groups=mesh['replica'=16,'tensor'=16] {'replica'}, dimensions={0}, use_global_device_ids=true | all-gather | bytes 243712 | tf_op jit(solution)/shard_map/all_gather | solution.py:61
  202.3 1.6 fusion.10
  203.9 5.4 %fusion.29 = f32[8,7,64,64]{2,3,1,0:T(8,128)S(1)} fusion(f32[8,7,64,64]{3,2,1,0:T(8,128)S(1)} %fusion.10, f32[64]{0:T(128)S(1)} %add_multiply_fusion, pred[64]{0:T(512)(128)(4,1)S(1)} %iota_compare_fusion.6), kind=kOutput, calls=%fused_computation.43 | convolution fusion | flops 176181248 | bytes 1835328 | tf_op jit(solution)/shard_map/ackj,jm->ackm/dot_general | solution.py:21
  209.4 1.7 fusion.3
  212.3 41.0 %all-gather.2 = f32[128,7,64]{2,0,1:T(8,128)S(1)} all-gather(f32[8,7,64]{2,0,1:T(8,128)S(1)} %get-tuple-element.4), channel_id=4, replica_groups=mesh['replica'=16,'tensor'=16] {'replica'}, dimensions={0}, use_global_device_ids=true | all-gather | bytes 243712 | tf_op jit(solution)/shard_map/all_gather | solution.py:61
  253.2 1.6 fusion.8
  254.9 5.4 %fusion.26 = f32[8,7,64,64]{2,3,1,0:T(8,128)S(1)} fusion(f32[8,7,64,64]{3,2,1,0:T(8,128)S(1)} %fusion.8, f32[64]{0:T(128)S(1)} %add_multiply_fusion, pred[64]{0:T(512)(128)(4,1)S(1)} %iota_compare_fusion.6), kind=kOutput, calls=%fused_computation.40 | convolution fusion | flops 176181248 | bytes 1835328 | tf_op jit(solution)/shard_map/ackj,jm->ackm/dot_general | solution.py:21
  260.3 1.7 fusion.4
  263.2 43.8 %all-gather.3 = f32[128,7,64]{2,0,1:T(8,128)S(1)} all-gather(f32[8,7,64]{2,0,1:T(8,128)S(1)} %get-tuple-element.6), channel_id=5, replica_groups=mesh['replica'=16,'tensor'=16] {'replica'}, dimensions={0}, use_global_device_ids=true | all-gather | bytes 243712 | tf_op jit(solution)/shard_map/all_gather | solution.py:61
  307.0 1.6 fusion.6
  308.6 5.4 %fusion.23 = f32[8,7,64,64]{2,3,1,0:T(8,128)S(1)} fusion(f32[8,7,64,64]{3,2,1,0:T(8,128)S(1)} %fusion.6, f32[64]{0:T(128)S(1)} %add_multiply_fusion, pred[64]{0:T(512)(128)(4,1)S(1)} %iota_compare_fusion.6), kind=kOutput, calls=%fused_computation.37 | convolution fusion | flops 176181248 | bytes 1835328 | tf_op jit(solution)/shard_map/ackj,jm->ackm/dot_general | solution.py:21
  314.1 1.7 fusion.5
  317.0 0.8 fusion.35
  317.7 4.3 %multiply_bitcast_fusion = f32[32,64,7,64]{1,0,3,2:T(8,128)} fusion(f32[32,7,64]{2,0,1:T(8,128)S(1)} %copy-done.5, f32[32,7,64]{0,2,1:T(8,128)S(1)} %fusion.35), kind=kLoop, calls=%fused_computation.2 | loop fusion | flops 917504 | bytes 3784704 | tf_op jit(solution)/shard_map/acn,acm->ancm/transpose | solution.py:55
  322.1 7.5 %reshape.51 = f32[2048,448]{0,1:T(8,128)} reshape(f32[32,64,7,64]{1,0,3,2:T(8,128)} %multiply_bitcast_fusion) | data formatting | bytes 7340032 | tf_op jit(solution)/shard_map/reshape | solution.py:56
  329.6 1.5 pad_maximum_fusion
  331.1 1.2 copy-done.2
  332.3 4.8 %subtract_bitcast_fusion = f32[1,2048,448]{1,2,0:T(8,128)} fusion(f32[2048,448]{0,1:T(8,128)S(1)} %copy-done.2, f32[2048,448]{0,1:T(8,128)} %reshape.51), kind=kLoop, calls=%fused_computation.4 | loop fusion | flops 917504 | bytes 11010048 | tf_op jit(solution)/shard_map/broadcast_in_dim | solution.py:56
  337.0 1.8 convert_element_type.2
  (39 shorter events, 6.7 us)
Async XLA Ops:
  7.2 1.5 copy-start
  7.2 52.8 %all-gather.6.cloned.1.call-start = ((), (), s32[]{:S(2)}) async-start(), calls=%async_computation.2 | async-start | bytes 4456448 | tf_op jit(solution)/shard_map/all_gather | solution.py:35
  7.9 329.1 %reduce-scatter.2.cloned.1.call-start = ((), (), s32[]{:S(2)}) async-start(), calls=%async_computation.1 | async-start | bytes 8912896 | tf_op jit(solution)/shard_map/reduce_scatter | solution.py:31
  15.5 0.8 copy-start.3
  15.5 44.5 %copy-start.6 = (bf16[1024,448]{0,1:T(8,128)(2,1)S(1)}, bf16[1024,448]{0,1:T(8,128)(2,1)}, u32[]{:S(2)}) copy-start(bf16[1024,448]{0,1:T(8,128)(2,1)} %param.6) | copy-start | bytes 2752516
  17.4 73.8 %copy-start.4 = (f32[32,7,64]{2,0,1:T(8,128)}, f32[32,7,64]{2,0,1:T(8,128)S(1)}, u32[]{:S(2)}) copy-start(f32[32,7,64]{2,0,1:T(8,128)S(1)} %fusion.20) | copy-start | bytes 172036
  315.8 2.0 copy-start.5
  329.6 2.7 copy-start.2
  332.3 6.5 %copy-start.1 = (bf16[2048,448]{0,1:T(8,128)(2,1)S(1)}, bf16[2048,448]{0,1:T(8,128)(2,1)}, u32[]{:S(2)}) copy-start(bf16[2048,448]{0,1:T(8,128)(2,1)} %param.7) | copy-start | bytes 5505028
Sparse Core Ops, SparseCore 0:
  9.8 50.1 all-gather.5
  62.5 100.8 reduce-scatter.1
where the time goes:
time: 351 us; the launch traced here: 346 us
  blocking collectives  180 us (51%)
  matrix products  72.6 us (21%)
  waiting for transfers between devices  42.4 us (12%)
  local copies, waits for them, and re-layouts  23.5 us (7%)
  between operations  14.5 us (4%)
  other arithmetic  13.2 us (4%)
    all_gather x4, blocking collectives, body(): gathered = lax.all_gather(block_rows[None], 'replica', axis=0, tiled=True)  180 us
    all_gather x1, waiting for transfers between devices, body(): lax.all_gather(activations, 'tensor', axis=1, tiled=True)  41.7 us
    dot_general x4, matrix products, decode(): right_done = jnp.einsum('ackj,jm->ackm', summed, basis, precision=highest)  21.8 us
    dot_general x1, matrix products, body(): half_done = jnp.einsum('ancm,lm->ancl', tile_view, basis, precision=highest)  16.1 us
    reshape x1, local copies, waits for them, and re-layouts, body(): tile_view = kept.reshape(tile_rows, TILE, tile_cols, TILE)  7.87 us
    reshape x1, local copies, waits for them, and re-layouts, body(): momentum_out = (kept - removed.reshape(feature_count, hidden_count))[None]  7.48 us
    dot_general x1, matrix products, body(): lax.dot_general(lax.all_gather(activations, 'tensor', axis=1, tiled=True)...  7.29 us
  transfers between devices with their start and end apart: 2, of which 1 were waited for; matrix products, arithmetic and copies ran while one was open for 30% of the time, Pallas kernels for 0%

commit v1 on v0

--- a/solution.py
+++ b/solution.py
@@ -58,7 +58,12 @@
     results = []
     for block_index in range(4):
         block_rows = coeff_rows[block_index * band : (block_index + 1) * band]
-        gathered = lax.all_gather(block_rows[None], "replica", axis=0, tiled=True)
+        gathered = jnp.concatenate(
+            lax.all_to_all(
+                jnp.stack([block_rows[None]] * lax.axis_size("replica")), "replica", 0, 0
+            ),
+            axis=0,
+        )
         block_chosen = freq_rows[:, block_index * band : (block_index + 1) * band]
         results.append(decode(gathered, block_chosen, basis))
     update = jnp.concatenate(results, axis=0).astype(jnp.bfloat16)

time: 351 us -> 237 us (0.68)
  blocking collectives: 180 us -> 0 us
  starting transfers between devices: 0.08 us -> 30.7 us
  waiting for transfers between devices: 42.4 us -> 60 us
  local copies, waits for them, and re-layouts: 23.5 us -> 33.6 us
  other arithmetic: 13.2 us -> 19.7 us
    all_gather x4 -> x0, blocking collectives: 180 us -> none  [body(): gathered = lax.all_gather(block_rows[None], 'replica', axis=0, tiled=True)]
    all_to_all x0 -> x4, starting transfers between devices: none -> 30.6 us  [body(): lax.all_to_all(jnp.stack([block_rows[None]] * lax.axis_size('replica')),...]
    all_to_all x0 -> x4, waiting for transfers between devices: none -> 16.5 us  [body(): lax.all_to_all(jnp.stack([block_rows[None]] * lax.axis_size('replica')),...]
    reshape x4, local copies, waits for them, and re-layouts: 2.17 us -> 7.19 us  [decode(): return decoded.reshape(summed.shape[0] * TILE, summed.shape[1] * TILE)]
    all_to_all x0 -> x4, other arithmetic: none -> 4.83 us  [body(): lax.all_to_all(jnp.stack([block_rows[None]] * lax.axis_size('replica')),...]
  transfers between devices with their start and end apart: 2 -> 6, of which waited for: 1 -> 3; matrix products, arithmetic and copies ran while one was open for 30% -> 53% of each run, Pallas kernels for 0% -> 0%
where the time goes in v1:
time: 237 us; the launch traced here: 232 us
  matrix products  73.7 us (31%)
  waiting for transfers between devices  60 us (25%)
  local copies, waits for them, and re-layouts  33.6 us (14%)
  starting transfers between devices  30.7 us (13%)
  other arithmetic  19.7 us (8%)
  between operations  14.7 us (6%)
    all_gather x1, waiting for transfers between devices, body(): lax.all_gather(activations, 'tensor', axis=1, tiled=True)  42.8 us
    all_to_all x4, starting transfers between devices, body(): lax.all_to_all(jnp.stack([block_rows[None]] * lax.axis_size('replica')),...  30.6 us
    dot_general x4, matrix products, decode(): right_done = jnp.einsum('ackj,jm->ackm', summed, basis, precision=highest)  22 us
    all_to_all x4, waiting for transfers between devices, body(): lax.all_to_all(jnp.stack([block_rows[None]] * lax.axis_size('replica')),...  16.5 us
    dot_general x1, matrix products, body(): half_done = jnp.einsum('ancm,lm->ancl', tile_view, basis, precision=highest)  16.3 us
    reshape x1, local copies, waits for them, and re-layouts, body(): tile_view = kept.reshape(tile_rows, TILE, tile_cols, TILE)  7.58 us
    reshape x1, local copies, waits for them, and re-layouts, body(): momentum_out = (kept - removed.reshape(feature_count, hidden_count))[None]  7.5 us
    dot_general x1, matrix products, body(): lax.dot_general(lax.all_gather(activations, 'tensor', axis=1, tiled=True)...  7.28 us
  transfers between devices with their start and end apart: 6, of which 3 were waited for; matrix products, arithmetic and copies ran while one was open for 53% of the time, Pallas kernels for 0%

profile of v1, /device:TPU:8, one launch (start us, length us, event | category | flops | bytes accessed | tf_op | source)
XLA Modules:
  0.0 232.3 jit_solution(13450982393267128027)
XLA Ops:
  8.7 6.8 %fusion.132 = f32[1024,2048]{1,0:T(8,128)} fusion(bf16[1024,448]{0,1:T(8,128)(2,1)} %param.6, bf16[2048,448]{0,1:T(8,128)(2,1)S(1)} %copy-done), kind=kOutput, calls=%fused_computation.155 | convolution fusion | flops 1879048192 | bytes 11141120 | tf_op jit(solution)/shard_map/dot_general | solution.py:28
  17.1 42.8 %all-gather.2.cloned.1.call-done = bf16[1024,2048]{1,0:T(8,128)(2,1)} async-done(((bf16[1024,128]{1,0:T(8,128)(2,1)}), bf16[1024,2048]{1,0:T(8,128)(2,1)}) %all-gather.2.cloned.1.call-update) | async-done | bytes 4194320 | tf_op jit(solution)/shard_map/all_gather | solution.py:35
  59.9 7.3 %bitcast_add_fusion = f32[2048,448]{0,1:T(8,128)} fusion(f32[1,2048,448]{1,2,0:T(8,128)} %param.8, bf16[1024,448]{0,1:T(8,128)(2,1)S(1)} %copy-done.3, bf16[1024,2048]{1,0:T(8,128)(2,1)} %all-gather.2.cloned.1.call-done), kind=kOutput, calls=%fused_computation.3 | convolution fusion | flops 1880883200 | bytes 12451840 | tf_op jit(solution)/shard_map/dot_general | solution.py:34
  67.2 7.6 %reshape.70 = f32[32,64,7,64]{1,0,3,2:T(8,128)} reshape(f32[2048,448]{0,1:T(8,128)} %bitcast_add_fusion) | data formatting | bytes 7340032 | tf_op jit(solution)/shard_map/reshape | solution.py:47
  74.8 16.3 %fusion = f32[32,64,7,64]{3,1,2,0:T(8,128)S(1)} fusion(f32[32,64,7,64]{1,0,3,2:T(8,128)} %reshape.70, f32[64]{0:T(128)S(1)} %add_multiply_fusion, pred[64]{0:T(512)(128)(4,1)S(1)} %iota_compare_fusion.10), kind=kOutput, calls=%fused_computation | convolution fusion | flops 704663552 | bytes 7340352 | tf_op jit(solution)/shard_map/ancm,lm->ancl/dot_general | solution.py:48
  91.1 6.2 %fusion.22 = f32[32,7,1,64]{3,2,1,0:T(1,128)S(1)} fusion(f32[32,64,7,64]{3,1,2,0:T(8,128)S(1)} %fusion, f32[32,7,64,1]{2,0,1,3:T(8,128)S(1)} %bitcast.112), kind=kOutput, calls=%fused_computation.35 | convolution fusion | flops 11010048 | bytes 3784704 | tf_op jit(solution)/shard_map/acn,ancl->acl/dot_general | solution.py:53
  98.4 10.0 %all-to-all-start = ((f32[16,1,3584]{2,1,0:T(1,128)}), f32[16,1,3584]{2,1,0:T(1,128)S(1)}, u32[]{:S(2)}, u32[]{:S(2)}) async-start(f32[16,1,3584]{2,1,0:T(1,128)} %reshape.90), calls=%async_computation.1 | async-start | bytes 458752 | tf_op jit(solution)/shard_map/all_to_all | solution.py:62
  109.5 12.7 %all-to-all-done = f32[16,1,3584]{2,1,0:T(1,128)S(1)} async-done(((f32[16,1,3584]{2,1,0:T(1,128)}), f32[16,1,3584]{2,1,0:T(1,128)S(1)}, u32[]{:S(2)}, u32[]{:S(2)}) %all-to-all-start) | async-done | bytes 229408 | tf_op jit(solution)/shard_map/all_to_all | solution.py:62
  122.1 5.0 %all-to-all-start.1 = ((f32[16,1,3584]{2,1,0:T(1,128)}), f32[16,1,3584]{2,1,0:T(1,128)S(1)}, u32[]{:S(2)}, u32[]{:S(2)}) async-start(f32[16,1,3584]{2,1,0:T(1,128)} %reshape.88), calls=%async_computation.2 | async-start | bytes 458752 | tf_op jit(solution)/shard_map/all_to_all | solution.py:62
  129.9 4.3 %multiply_bitcast_fusion = f32[32,64,7,64]{1,0,3,2:T(8,128)} fusion(f32[32,7,64]{2,0,1:T(8,128)S(1)} %fusion.24, f32[32,7,64]{0,2,1:T(8,128)S(1)} %fusion.39), kind=kLoop, calls=%fused_computation.2 | loop fusion | flops 917504 | bytes 3784704 | tf_op jit(solution)/shard_map/acn,acm->ancm/transpose | solution.py:55
  134.2 7.5 %reshape.71 = f32[2048,448]{0,1:T(8,128)} reshape(f32[32,64,7,64]{1,0,3,2:T(8,128)} %multiply_bitcast_fusion) | data formatting | bytes 7340032 | tf_op jit(solution)/shard_map/reshape | solution.py:56
  141.7 9.6 %all-to-all-start.2 = ((f32[16,1,3584]{2,1,0:T(1,128)}), f32[16,1,3584]{2,1,0:T(1,128)S(1)}, u32[]{:S(2)}, u32[]{:S(2)}) async-start(f32[16,1,3584]{2,1,0:T(1,128)} %reshape.86), calls=%async_computation.3 | async-start | bytes 458752 | tf_op jit(solution)/shard_map/all_to_all | solution.py:62
  151.3 6.0 %subtract_bitcast_fusion = f32[1,2048,448]{1,2,0:T(8,128)} fusion(f32[2048,448]{0,1:T(8,128)} %bitcast_add_fusion, f32[2048,448]{0,1:T(8,128)} %reshape.71), kind=kLoop, calls=%fused_computation.4 | loop fusion | flops 917504 | bytes 11010048 | tf_op jit(solution)/shard_map/broadcast_in_dim | solution.py:56
  160.6 3.8 %all-to-all-done.2 = f32[16,1,3584]{2,1,0:T(1,128)S(1)} async-done(((f32[16,1,3584]{2,1,0:T(1,128)}), f32[16,1,3584]{2,1,0:T(1,128)S(1)}, u32[]{:S(2)}, u32[]{:S(2)}) %all-to-all-start.2) | async-done | bytes 229408 | tf_op jit(solution)/shard_map/all_to_all | solution.py:62
  164.4 6.0 %all-to-all-start.3 = ((f32[16,1,3584]{2,1,0:T(1,128)}), f32[16,1,3584]{2,1,0:T(1,128)S(1)}, u32[]{:S(2)}, u32[]{:S(2)}) async-start(f32[16,1,3584]{2,1,0:T(1,128)} %reshape.84), calls=%async_computation.4 | async-start | bytes 458752 | tf_op jit(solution)/shard_map/all_to_all | solution.py:62
  171.7 1.8 fusion.12
  173.5 1.8 fusion.10
  175.2 1.8 fusion.8
  177.0 5.4 %fusion.36 = f32[8,7,64,64]{2,3,1,0:T(8,128)S(1)} fusion(f32[8,7,64,64]{3,2,1,0:T(8,128)S(1)} %fusion.12, f32[64]{0:T(128)S(1)} %add_multiply_fusion, pred[64]{0:T(512)(128)(4,1)S(1)} %iota_compare_fusion.10), kind=kOutput, calls=%fused_computation.50 | convolution fusion | flops 176181248 | bytes 1835328 | tf_op jit(solution)/shard_map/ackj,jm->ackm/dot_general | solution.py:21
  182.5 1.7 fusion.2
  184.2 5.6 %fusion.33 = f32[8,7,64,64]{2,3,1,0:T(8,128)S(1)} fusion(f32[8,7,64,64]{3,2,1,0:T(8,128)S(1)} %fusion.10, f32[64]{0:T(128)S(1)} %add_multiply_fusion, pred[64]{0:T(512)(128)(4,1)S(1)} %iota_compare_fusion.10), kind=kOutput, calls=%fused_computation.47 | convolution fusion | flops 176181248 | bytes 1835328 | tf_op jit(solution)/shard_map/ackj,jm->ackm/dot_general | solution.py:21
  189.8 5.4 %fusion.30 = f32[8,7,64,64]{2,3,1,0:T(8,128)S(1)} fusion(f32[8,7,64,64]{3,2,1,0:T(8,128)S(1)} %fusion.8, f32[64]{0:T(128)S(1)} %add_multiply_fusion, pred[64]{0:T(512)(128)(4,1)S(1)} %iota_compare_fusion.10), kind=kOutput, calls=%fused_computation.44 | convolution fusion | flops 176181248 | bytes 1835328 | tf_op jit(solution)/shard_map/ackj,jm->ackm/dot_general | solution.py:21
  195.3 1.7 fusion.3
  197.0 1.5 copy.37
  198.6 1.8 reshape.73
  201.9 2.7 %reshape.75 = bf16[512,448]{0,1:T(8,128)(2,1)} reshape(bf16[8,64,7,64]{1,0,3,2:T(8,128)(2,1)} %copy.41) | data formatting | bytes 917504 | tf_op jit(solution)/shard_map/reshape | solution.py:23
  204.6 1.7 fusion.4
  209.6 1.8 fusion.6
  211.4 5.4 %fusion.27 = f32[8,7,64,64]{2,3,1,0:T(8,128)S(1)} fusion(f32[8,7,64,64]{3,2,1,0:T(8,128)S(1)} %fusion.6, f32[64]{0:T(128)S(1)} %add_multiply_fusion, pred[64]{0:T(512)(128)(4,1)S(1)} %iota_compare_fusion.10), kind=kOutput, calls=%fused_computation.41 | convolution fusion | flops 176181248 | bytes 1835328 | tf_op jit(solution)/shard_map/ackj,jm->ackm/dot_general | solution.py:21
  216.9 1.7 fusion.5
  220.5 2.7 %pad_maximum_fusion = bf16[2048,448]{0,1:T(8,128)(2,1)} fusion(bf16[512,448]{0,1:T(8,128)(2,1)} %reshape.79, bf16[512,448]{0,1:T(8,128)(2,1)} %reshape.77, bf16[512,448]{0,1:T(8,128)(2,1)} %reshape.75, bf16[512,448]{0,1:T(8,128)(2,1)S(1)} %reshape.73), kind=kLoop, calls=%fused_computation.5 | loop fusion | flops 7340032 | bytes 3670016 | tf_op jit(solution)/shard_map/concatenate | solution.py:69
  223.3 1.8 convert_element_type.2
  (50 shorter events, 19.3 us)
Async XLA Ops:
  7.2 1.5 copy-start
  7.2 52.8 %all-gather.2.cloned.1.call-start = ((), (), s32[]{:S(2)}) async-start(), calls=%async_computation.6 | async-start | bytes 4456448 | tf_op jit(solution)/shard_map/all_gather | solution.py:35
  7.9 215.4 %reduce-scatter.2.cloned.1.call-start = ((), (), s32[]{:S(2)}) async-start(), calls=%async_computation.5 | async-start | bytes 8912896 | tf_op jit(solution)/shard_map/reduce_scatter | solution.py:31
  15.5 0.8 copy-start.2
  15.5 44.5 %copy-start.3 = (bf16[1024,448]{0,1:T(8,128)(2,1)S(1)}, bf16[1024,448]{0,1:T(8,128)(2,1)}, u32[]{:S(2)}) copy-start(bf16[1024,448]{0,1:T(8,128)(2,1)} %param.6) | copy-start | bytes 2752516
  98.4 23.7 %all-to-all-start = ((f32[16,1,3584]{2,1,0:T(1,128)}), f32[16,1,3584]{2,1,0:T(1,128)S(1)}, u32[]{:S(2)}, u32[]{:S(2)}) async-start(f32[16,1,3584]{2,1,0:T(1,128)} %reshape.90), calls=%async_computation.1 | async-start | bytes 458752 | tf_op jit(solution)/shard_map/all_to_all | solution.py:62
  122.1 19.6 %all-to-all-start.1 = ((f32[16,1,3584]{2,1,0:T(1,128)}), f32[16,1,3584]{2,1,0:T(1,128)S(1)}, u32[]{:S(2)}, u32[]{:S(2)}) async-start(f32[16,1,3584]{2,1,0:T(1,128)} %reshape.88), calls=%async_computation.2 | async-start | bytes 458752 | tf_op jit(solution)/shard_map/all_to_all | solution.py:62
  141.7 22.7 %all-to-all-start.2 = ((f32[16,1,3584]{2,1,0:T(1,128)}), f32[16,1,3584]{2,1,0:T(1,128)S(1)}, u32[]{:S(2)}, u32[]{:S(2)}) async-start(f32[16,1,3584]{2,1,0:T(1,128)} %reshape.86), calls=%async_computation.3 | async-start | bytes 458752 | tf_op jit(solution)/shard_map/all_to_all | solution.py:62
  164.4 43.9 %all-to-all-start.3 = ((f32[16,1,3584]{2,1,0:T(1,128)}), f32[16,1,3584]{2,1,0:T(1,128)S(1)}, u32[]{:S(2)}, u32[]{:S(2)}) async-start(f32[16,1,3584]{2,1,0:T(1,128)} %reshape.84), calls=%async_computation.4 | async-start | bytes 458752 | tf_op jit(solution)/shard_map/all_to_all | solution.py:62
  219.2 5.9 %copy-start.1 = (bf16[2048,448]{0,1:T(8,128)(2,1)S(1)}, bf16[2048,448]{0,1:T(8,128)(2,1)}, u32[]{:S(2)}) copy-start(bf16[2048,448]{0,1:T(8,128)(2,1)} %param.7) | copy-start | bytes 5505028
Sparse Core Ops, SparseCore 0:
  9.8 50.1 all-gather.1
  62.5 120.4 reduce-scatter.1
